TPU v7x, 512 devices: a whole 4x4x16 slice. The times are simulated.
512 devices in a mesh: layer: 64 (over x_lo, z, core), rep: 8 (over y, x_hi).
Axes of the slice: x: 4 (x_hi: 2, x_lo: 2; x = x_hi * 2 + x_lo), y: 4, z: 16, core: 2. Of those that a mesh axis runs over, the one named last changes fastest.
Arguments:
- gradients: bfloat16 [8, 64, 512, 1024], P('rep', 'layer'), may hold values from -60 to 60
- inverse_out: bfloat16 [64, 512, 512], P('layer', 'rep'), may hold values from -1 to 4
- inverse_in: bfloat16 [64, 1024, 1024], P('layer', 'rep'), may hold values from -1 to 4
- cross_out: bfloat16 [64, 512, 512], P('layer', 'rep'), may hold values from -0.125 to 0.125
- cross_in: bfloat16 [64, 1024, 1024], P('layer', 'rep'), may hold values from -0.1875 to 0.1875
- momentum: float32 [64, 512, 1024], P('layer', 'rep'), may hold values from -3 to 3
Outputs:
- momentum_new: float32 [64, 512, 1024], P('layer', 'rep')
All inputs are finite; a program needn't handle non-finite values.
Results may differ from a plain program's by a relative error of at most 0.003.
Values may be sent and summed in bfloat16 or wider, within the bound.
A program may use at most 64 MiB of HBM per device.

v0:
```python
import jax
import jax.numpy as jnp
from jax import lax
from jax.sharding import PartitionSpec as P


def passed_along(value, axis, steps):
    count = lax.axis_size(axis)
    initial, last = (max(0, -steps), min(count, count - steps))
    return lax.ppermute(value, axis, [(source, source + steps) for source in range(initial, last)])


def in_order(tiles, dim):
    shape = list(tiles.shape[1:])
    shape[dim] *= tiles.shape[0]
    return jnp.moveaxis(tiles, 0, dim).reshape(shape)


def gather_together(arrays, axis, dims):
    line = jnp.concatenate([a.reshape(-1) for a in arrays])
    lines, at, gathered = (lax.all_gather(line, axis), 0, [])
    for a, dim in zip(arrays, dims):
        tiles = lines[:, at : at + a.size].reshape(-1, *a.shape)
        gathered.append(in_order(tiles, dim))
        at += a.size
    return tuple(gathered)


def in_blocks(shard, dim, peers):
    shape = shard.shape
    tiles = shard.reshape(*shape[:dim], peers, shape[dim] // peers, *shape[dim + 1 :])
    return jnp.moveaxis(tiles, dim, 0)


def summed_on_arrival(shard, axis, dim):
    peers = lax.axis_size(axis)
    tiles = lax.all_to_all(in_blocks(shard, dim, peers), axis, 0, 0, tiled=True)
    return jnp.sum(tiles, axis=0)


def body(gradients, inverse_out, inverse_in, cross_out, cross_in, momentum):
    own_block = gradients[0, 0]
    following = passed_along(own_block, "layer", -1)
    inv_left, inv_right, cross_left, cross_right = gather_together(
        (inverse_out[0], inverse_in[0], cross_out[0], cross_in[0]), "rep", (0, 0, 0, 0)
    )
    first = jnp.dot(cross_left, following, preferred_element_type=jnp.float32).astype(jnp.bfloat16)
    cross_term = jnp.dot(first, cross_right, preferred_element_type=jnp.float32)
    residual = (own_block.astype(jnp.float32) - cross_term).astype(jnp.bfloat16)
    left_applied = jnp.dot(inv_left, residual, preferred_element_type=jnp.float32).astype(
        jnp.bfloat16
    )
    precond = jnp.dot(left_applied, inv_right, preferred_element_type=jnp.float32).astype(
        jnp.bfloat16
    )
    back_product = lax.dot_general(
        cross_left, precond, (((0,), (0,)), ((), ())), preferred_element_type=jnp.float32
    ).astype(jnp.bfloat16)
    correction = lax.dot_general(
        back_product, cross_right, (((1,), (1,)), ((), ())), preferred_element_type=jnp.float32
    ).astype(jnp.bfloat16)
    incoming = passed_along(correction, "layer", 1)
    update = precond.astype(jnp.float32) - incoming.astype(jnp.float32)
    delta = update * lax.rsqrt(jnp.mean(update * update) + 1e-06)
    share = summed_on_arrival(delta, "rep", 0)
    replica_count = lax.axis_size("rep")
    renewed = 0.9 * momentum[0] + share * (1.0 / replica_count)
    return renewed[None]


def solution(mesh):
    in_specs = (
        P("rep", "layer", None, None),
        P("layer", "rep", None),
        P("layer", "rep", None),
        P("layer", "rep", None),
        P("layer", "rep", None),
        P("layer", "rep", None),
    )
    out_specs = P("layer", "rep", None)
    return jax.shard_map(body, mesh=mesh, in_specs=in_specs, out_specs=out_specs, check_vma=False)
```

profile of v0, /device:TPU:2, one launch (start us, length us, event | category | flops | bytes accessed | tf_op | source)
XLA Modules:
  0.0 200.9 jit_solution(13488653658408383222)
XLA Ops:
  6.5 0.0 all-gather.3.cloned.1.call-start
  6.5 0.9 copy.7
  7.4 0.9 copy.9
  8.3 1.0 copy.8
  9.3 1.0 copy.10
  10.3 0.9 pad_maximum_fusion
  11.2 0.0 all-gather.3.cloned.1.call-update
  11.2 10.8 %collective-permute-start = (bf16[512,1024]{1,0:T(8,128)(2,1)}, bf16[512,1024]{1,0:T(8,128)(2,1)}, u32[]{:S(2)}, u32[]{:S(2)}) collective-permute-start(bf16[512,1024]{1,0:T(8,128)(2,1)} %bitcast), channel_id=1, source_target_pairs={{8,0},{16,8},{24,16},{32,24},{40,32},{48,40},{56,48},{64,56},{72,6... | collective-permute-start | bytes 3145736 | tf_op jit(solution)/shard_map/ppermute | solution.py:10
  22.0 88.1 %all-gather.3.cloned.1.call-done = bf16[2621440]{0:T(1024)(128)(2,1)} async-done(((bf16[327680]{0:T(1024)(128)(2,1)}), bf16[2621440]{0:T(1024)(128)(2,1)}) %all-gather.3.cloned.1.call-update) | async-done | bytes 5242896 | tf_op jit(solution)/shard_map/all_gather | solution.py:21
  110.1 7.0 %reshape.13 = bf16[8,327680]{1,0:T(8,128)(2,1)} reshape(bf16[2621440]{0:T(1024)(128)(2,1)} %all-gather.3.cloned.1.call-done) | data formatting | bytes 10485760 | tf_op jit(solution)/shard_map/all_gather | solution.py:21
  117.1 3.8 %fusion.2 = (bf16[8,131072]{1,0:T(8,128)(2,1)}, bf16[8,131072]{1,0:T(8,128)(2,1)S(1)}) fusion(bf16[8,327680]{1,0:T(8,128)(2,1)} %reshape.13), kind=kLoop, calls=%fused_computation.12 | loop fusion | bytes 8388608 | tf_op jit(solution)/shard_map/slice | solution.py:23
  120.9 1.3 fusion.1
  122.2 3.9 %reshape_reshape.15 = bf16[1024,1024]{1,0:T(8,128)(2,1)} reshape(bf16[8,131072]{1,0:T(8,128)(2,1)} %get-tuple-element.7) | data formatting | bytes 4194304 | tf_op jit(solution)/shard_map/reshape;reshape | solution.py:16
  126.1 1.0 reshape_reshape.12
  127.1 1.1 reshape_reshape.13
  128.1 2.3 %reshape_reshape.14 = bf16[1024,1024]{1,0:T(8,128)(2,1)} reshape(bf16[8,131072]{1,0:T(8,128)(2,1)S(1)} %get-tuple-element.8) | data formatting | bytes 4194304 | tf_op jit(solution)/shard_map/reshape;reshape | solution.py:16
  130.4 0.0 copy-start
  130.4 0.0 collective-permute-done
  130.4 5.3 %subtract_convert_fusion = bf16[512,1024]{1,0:T(8,128)(2,1)} fusion(bf16[1024,1024]{1,0:T(8,128)(2,1)} %reshape_reshape.14, bf16[512,512]{1,0:T(8,128)(2,1)} %reshape_reshape.13, bf16[512,1024]{1,0:T(8,128)(2,1)} %collective-permute-done, bf16[1,1,512,1024]{3,2,1,0:T(8,128)(2,1)} %param.6), kind=kOutput, calls=%fused_computation.2 | convolution fusion | flops 1612709888 | bytes 5767168 | tf_op jit(solution)/shard_map/dot_general | solution.py:48
  135.7 0.0 copy-done
  135.7 3.2 %convolution_convert_fusion.1 = bf16[512,1024]{1,0:T(8,128)(2,1)S(1)} fusion(bf16[1024,1024]{1,0:T(8,128)(2,1)S(1)} %copy-done, bf16[512,512]{1,0:T(8,128)(2,1)} %reshape_reshape.12, bf16[512,1024]{1,0:T(8,128)(2,1)} %subtract_convert_fusion), kind=kOutput, calls=%fused_computation.5 | convolution fusion | flops 1611661312 | bytes 4718592 | tf_op jit(solution)/shard_map/dot_general | solution.py:53
  138.9 3.6 %convolution_convert_fusion = bf16[512,1024]{1,0:T(8,128)(2,1)S(1)} fusion(bf16[1024,1024]{1,0:T(8,128)(2,1)} %reshape_reshape.14, bf16[512,512]{1,0:T(8,128)(2,1)} %reshape_reshape.13, bf16[512,1024]{1,0:T(8,128)(2,1)S(1)} %convolution_convert_fusion.1), kind=kOutput, calls=%fused_computation.4 | convolution fusion | flops 1611661312 | bytes 4718592 | tf_op jit(solution)/shard_map/dot_general | solution.py:59
  142.5 1.9 collective-permute-start.1
  144.4 16.4 %collective-permute-done.1 = bf16[512,1024]{1,0:T(8,128)(2,1)S(1)} collective-permute-done((bf16[512,1024]{1,0:T(8,128)(2,1)S(1)}, bf16[512,1024]{1,0:T(8,128)(2,1)S(1)}, u32[]{:S(2)}, u32[]{:S(2)}) %collective-permute-start.1) | collective-permute-done | bytes 1048608 | tf_op jit(solution)/shard_map/ppermute | solution.py:10
  160.8 1.2 multiply_reduce_fusion
  162.7 0.4 fusion
  163.1 29.2 %all_to_all.5 = f32[8,64,1024]{2,1,0:T(8,128)S(1)} all-to-all(f32[8,64,1024]{2,1,0:T(8,128)S(1)} %bitcast.22), channel_id=1, replica_groups=mesh['layer'=64,'rep'=8] {'rep'}, dimensions={0} | all-to-all | bytes 4194304 | tf_op jit(solution)/shard_map/all_to_all | solution.py:37
  192.3 0.0 copy-start.1
  192.3 0.1 reduce_sum.19
  192.5 0.8 copy-done.1
  193.3 0.7 bitcast_add_fusion
Async XLA Ops:
  6.5 103.6 %all-gather.3.cloned.1.call-start = ((), (), s32[]{:S(2)}) async-start(), calls=%async_computation.1 | async-start | bytes 5898240 | tf_op jit(solution)/shard_map/all_gather | solution.py:21
  11.2 119.2 %collective-permute-start = (bf16[512,1024]{1,0:T(8,128)(2,1)}, bf16[512,1024]{1,0:T(8,128)(2,1)}, u32[]{:S(2)}, u32[]{:S(2)}) collective-permute-start(bf16[512,1024]{1,0:T(8,128)(2,1)} %bitcast), channel_id=1, source_target_pairs={{8,0},{16,8},{24,16},{32,24},{40,32},{48,40},{56,48},{64,56},{72,6... | collective-permute-start | bytes 3145736 | tf_op jit(solution)/shard_map/ppermute | solution.py:10
  130.4 5.3 %copy-start = (bf16[1024,1024]{1,0:T(8,128)(2,1)S(1)}, bf16[1024,1024]{1,0:T(8,128)(2,1)}, u32[]{:S(2)}) copy-start(bf16[1024,1024]{1,0:T(8,128)(2,1)} %reshape_reshape.15) | copy-start | bytes 6291460
  142.5 18.3 %collective-permute-start.1 = (bf16[512,1024]{1,0:T(8,128)(2,1)S(1)}, bf16[512,1024]{1,0:T(8,128)(2,1)S(1)}, u32[]{:S(2)}, u32[]{:S(2)}) collective-permute-start(bf16[512,1024]{1,0:T(8,128)(2,1)S(1)} %convolution_convert_fusion), channel_id=1, source_target_pairs={{0,8},{8,16},{16,24},{24,32},{32,40},{40,48},{48,56},{56,64},{64,7... | collective-permute-start | bytes 3145736 | tf_op jit(solution)/shard_map/ppermute | solution.py:10
  192.3 1.0 copy-start.1
Sparse Core Ops, SparseCore 0:
  11.3 98.7 all-gather.2
where the time goes:
time: 202 us; the launch traced here: 201 us
  waiting for transfers between devices  104 us (51%)
  blocking collectives  29.2 us (14%)
  local copies, waits for them, and re-layouts  24.8 us (12%)
  between operations  14.2 us (7%)
  starting transfers between devices  12.7 us (6%)
  matrix products  12 us (6%)
  other arithmetic  3.41 us (2%)
    all_gather x1, waiting for transfers between devices, gather_together(): lines, at, gathered = (lax.all_gather(line, axis), 0, [])  88.1 us
    all_to_all x1, blocking collectives, summed_on_arrival(): tiles = lax.all_to_all(in_blocks(shard, dim, peers), axis, 0, 0, tiled=True)  29.2 us
    ppermute x2, waiting for transfers between devices, passed_along(): lax.ppermute(value, axis, [(source, source + steps) for source in range(i...  16.4 us
    ppermute x2, starting transfers between devices, passed_along(): lax.ppermute(value, axis, [(source, source + steps) for source in range(i...  12.7 us
    another operation x4, local copies, waits for them, and re-layouts, in_order(): return jnp.moveaxis(tiles, 0, dim).reshape(shape)  8.21 us
    all_gather x1, local copies, waits for them, and re-layouts, gather_together(): lines, at, gathered = (lax.all_gather(line, axis), 0, [])  7.01 us
    dot_general x1, matrix products, body(): cross_term = jnp.dot(first, cross_right, preferred_element_type=jnp.float32)  5.25 us
    slice x2, local copies, waits for them, and re-layouts, gather_together(): tiles = lines[:, at:at + a.size].reshape(-1, *a.shape)  5.09 us
  transfers between devices with their start and end apart: 3, of which 2 were waited for; matrix products, arithmetic and copies ran while one was open for 10% of the time, Pallas kernels for 0%

commit v1 on v0

v1 whole, which is shorter than its diff:
```python
import functools

import jax
import jax.numpy as jnp
from jax import lax
from jax.experimental import pallas as pl
from jax.experimental.pallas import tpu as pltpu
from jax.sharding import PartitionSpec as P

MESH = pl.DeviceIdType.MESH
RING = 4
CHUNKS = 4
PER_ARRAY = 18
BF = jnp.bfloat16
F32 = jnp.float32


def dot(a, b):
    return jnp.dot(a, b, preferred_element_type=F32)


def dot_t(a, b):
    return lax.dot_general(a, b, (((1,), (1,)), ((), ())), preferred_element_type=F32)


def kernel(
    layers, reps, own_g, sh_o, sh_i, sh_x, sh_y, sh_m, out,
    f_x, f_y, f_o, f_i, xt, g_own, g_next, first, resid, left, acc, pre, back, corr, inc, ub, rb,
    sc_out, sc_in, mom, send, recv, loc,
):
    layer, rep = lax.axis_index("layer"), lax.axis_index("rep")
    y, xh = rep // 2, rep % 2
    d_out, d_in = g_own.shape
    slab = d_out // reps

    def slot_of(dy, other):
        return ((y + dy + RING) % RING) * 2 + ((1 - xh) if other else xh)

    up, down, across = (layer, slot_of(1, False)), (layer, slot_of(-1, False)), (layer, slot_of(0, True))

    local = []

    def bring(src, dst):
        c = pltpu.make_async_copy(src, dst, loc.at[len(local)])
        c.start()
        local.append(c)

    arrays = {"x": (sh_x, f_x), "y": (sh_y, f_y), "o": (sh_o, f_o), "i": (sh_i, f_i)}

    def rows_of(q, slot, part=None):
        shard, full = arrays[q]
        n = shard.shape[0]
        cols = full.shape[1]
        cut = cols * 3 // 4
        lo, size = {"a": (0, cut), "b": (cut, cols - cut), None: (0, cols)}[part]
        return n, lo, size

    def full_at(q, slot, part, half=None):
        n, lo, size = rows_of(q, slot, part)
        start, count = (0, n) if half is None else (half * (n // 2), n // 2)
        at = pl.multiple_of(slot * n + start, count)
        return arrays[q][1].at[pl.ds(at, count), pl.ds(lo, size)]

    def own_at(q, part):
        n, lo, size = rows_of(q, None, part)
        return arrays[q][0].at[pl.ds(0, n), pl.ds(lo, size)]

    for q in arrays:
        bring(arrays[q][0], full_at(q, rep, None))
    bring(own_g, g_own)
    bring(sh_m, mom)

    has_next = (layer + 1) // layers
    has_prev = (layer + layers - 1) // layers
    barrier = pltpu.get_barrier_semaphore()
    for k in range(1, reps):
        pl.semaphore_signal(barrier, inc=1, device_id=(layer, (rep + k) % reps), device_id_type=MESH)

    @pl.when(layer < layers - 1)
    def _():
        pl.semaphore_signal(barrier, inc=1, device_id=(layer + 1, rep), device_id_type=MESH)

    @pl.when(layer > 0)
    def _():
        pl.semaphore_signal(barrier, inc=1, device_id=(layer - 1, rep), device_id_type=MESH)

    pl.semaphore_wait(barrier, reps - 1 + (1 - has_next) + has_prev)

    copies = {}

    def remote(key, src, dst, device):
        i = len(copies)
        copies[key] = pltpu.make_async_remote_copy(
            src_ref=src, dst_ref=dst, send_sem=send.at[i], recv_sem=recv.at[i],
            device_id=device, device_id_type=MESH,
        )
        return copies[key]

    def put(key, src, dst, device):
        remote(key, src, dst, device).start()

    def got(*keys):
        for key in keys:
            copies[key].wait_recv()

    def begin(q):
        put((q, "ax"), own_at(q, "a"), full_at(q, rep, "a"), across)
        put((q, "bx0"), own_at(q, "b"), full_at(q, rep, "b"), across)
        put((q, "bu"), own_at(q, "b"), full_at(q, rep, "b"), up)
        put((q, "bd"), own_at(q, "b"), full_at(q, rep, "b"), down)
        put((q, "au"), own_at(q, "a"), full_at(q, rep, "a"), up)
        put((q, "ad"), own_at(q, "a"), full_at(q, rep, "a"), down)

    def pass_on(q, name, slot, part, device, half=None):
        ref = full_at(q, slot, part, half)
        put((q, name), ref, ref, device)

    def stage1(q):
        got((q, "bu"))
        pass_on(q, "bur", slot_of(-1, False), "b", up, 0)
        pass_on(q, "bx1", slot_of(-1, False), "b", across)
        got((q, "bd"))
        pass_on(q, "bdr", slot_of(1, False), "b", down, 1)
        pass_on(q, "bx2", slot_of(1, False), "b", across)
        got((q, "ax"))
        pass_on(q, "pu", slot_of(0, True), "a", up)
        pass_on(q, "pd", slot_of(0, True), "a", down)

    def stage2(q):
        got((q, "au"))
        pass_on(q, "aur", slot_of(-1, False), "a", up, 0)
        got((q, "ad"))
        pass_on(q, "adr", slot_of(1, False), "a", down, 1)
        got((q, "bur"))
        pass_on(q, "bx3", slot_of(2, False), "b", across, 0)
        got((q, "bdr"))
        pass_on(q, "bx4", slot_of(2, False), "b", across, 1)

    def stage3(q):
        got((q, "pu"))
        pass_on(q, "pur", slot_of(-1, True), "a", up, 0)
        got((q, "pd"))
        pass_on(q, "pdr", slot_of(1, True), "a", down, 1)

    def finish(q):
        for k in ("bx0", "bx1", "bx2", "aur", "adr", "bx3", "bx4", "pur", "pdr"):
            got((q, k))

    tile = d_in // CHUNKS

    def each_tile(body):
        @pl.loop(0, CHUNKS)
        def _(n):
            body(pl.ds(pl.multiple_of(n * tile, tile), tile))

    for q in "xyo":
        begin(q)
    forward = remote("g", own_g, g_next, (lax.max(layer - 1, 0), rep))

    @pl.when(layer > 0)
    def _():
        forward.start()

    stage1("x")
    stage1("y")
    begin("i")
    stage1("o")
    for q in "xyo":
        stage2(q)
    for q in "xyo":
        stage3(q)
    stage1("i")
    for c in local:
        c.wait()
    finish("x")
    xt[...] = f_x[...].T

    @pl.when(layer < layers - 1)
    def _():
        forward.wait_recv()

    @pl.when(layer == layers - 1)
    def _():
        g_next[...] = jnp.zeros_like(g_next)

    def step1(cols):
        first[:, cols] = dot(f_x[...], g_next[:, cols]).astype(BF)

    each_tile(step1)
    stage2("i")
    finish("y")

    def step2(cols):
        resid[:, cols] = (g_own[:, cols].astype(F32) - dot(first[...], f_y[:, cols])).astype(BF)

    each_tile(step2)
    stage3("i")
    finish("o")

    def step3(cols):
        left[:, cols] = dot(f_o[...], resid[:, cols]).astype(BF)

    each_tile(step3)

    depth = 2 * sh_i.shape[0]

    def part(dy):
        return pl.ds(pl.multiple_of(((y + dy + RING) % RING) * depth, depth), depth)

    got(("i", "bx0"))

    def step4_own(cols):
        acc[:, cols] = dot(left[:, part(0)], f_i[part(0), cols])

    each_tile(step4_own)
    got(("i", "bx1"), ("i", "bx2"))

    def step4_near(cols):
        acc[:, cols] += dot(left[:, part(-1)], f_i[part(-1), cols]) + dot(left[:, part(1)], f_i[part(1), cols])

    each_tile(step4_near)
    for k in ("aur", "adr", "bx3", "bx4", "pur", "pdr"):
        got(("i", k))

    def step4_far(cols):
        pre[:, cols] = (acc[:, cols] + dot(left[:, part(2)], f_i[part(2), cols])).astype(BF)

    each_tile(step4_far)

    def step5(cols):
        back[:, cols] = dot(xt[...], pre[:, cols]).astype(BF)

    each_tile(step5)

    for c in range(CHUNKS):
        cols = pl.ds(c * tile, tile)
        corr[:, cols] = dot_t(back[...], f_y[cols, :]).astype(BF)
        hop = remote(("c", c), corr.at[:, cols], inc.at[:, cols], (lax.min(layer + 1, layers - 1), rep))

        @pl.when(layer < layers - 1)
        def _(hop=hop):
            hop.start()

    @pl.when(layer == 0)
    def _():
        inc[...] = jnp.zeros_like(inc)

    total = jnp.zeros((1, 1), F32)
    for c in range(CHUNKS):
        cols = pl.ds(c * tile, tile)

        @pl.when(layer > 0)
        def _(c=c):
            copies[("c", c)].wait_recv()

        update = pre[:, cols].astype(F32) - inc[:, cols].astype(F32)
        ub[:, cols] = update.astype(BF)
        total = total + jnp.sum(update * update, keepdims=True)
        if c == CHUNKS - 1:
            scale = lax.rsqrt(total * (1.0 / (d_out * d_in)) + 1e-06)
            sc_out[...] = jnp.broadcast_to(scale, sc_out.shape)
            for k in range(1, reps):
                put(("s", k), sc_out, sc_in.at[rep], (layer, (rep + k) % reps))
        for k in range(1, reps):
            to = (rep + k) % reps
            rows = pl.ds(pl.multiple_of(to * slab, slab), slab)
            put(("u", c, k), ub.at[rows, cols], rb.at[rep, :, cols], (layer, to))

    mine = pl.ds(pl.multiple_of(rep * slab, slab), slab)
    rb[rep] = ub[mine, :]
    sc_in[rep] = sc_out[...]
    for k in range(1, reps):
        got(("s", k))
    for c in range(CHUNKS):
        for k in range(1, reps):
            got(("u", c, k))
    share = rb[0].astype(F32) * sc_in[0, 0:1, 0:1]
    for r in range(1, reps):
        share = share + rb[r].astype(F32) * sc_in[r, 0:1, 0:1]
    out[...] = 0.9 * mom[...] + share * (1.0 / reps)

    for key, c in copies.items():
        if key == "g":
            pl.when(layer > 0)(c.wait_send)
        elif key[0] == "c":
            pl.when(layer < layers - 1)(c.wait_send)
        else:
            c.wait_send()


def solution(mesh):
    layers, reps = mesh.shape["layer"], mesh.shape["rep"]

    def body(gradients, inverse_out, inverse_in, cross_out, cross_in, momentum):
        g, m = gradients[0, 0], momentum[0]
        d_out, d_in = g.shape
        n_copies = 4 * PER_ARRAY + 1 + CHUNKS + (CHUNKS + 1) * (reps - 1)
        full = pltpu.VMEM((d_out, d_in), BF)
        small, large = pltpu.VMEM((d_out, d_out), BF), pltpu.VMEM((d_in, d_in), BF)
        done = pl.pallas_call(
            functools.partial(kernel, layers, reps),
            out_shape=jax.ShapeDtypeStruct(m.shape, F32),
            in_specs=[pl.BlockSpec(memory_space=pl.ANY)] * 6,
            out_specs=pl.BlockSpec(memory_space=pltpu.VMEM),
            scratch_shapes=[
                small, large, small, large, small,
                full, full, full, full, full, pltpu.VMEM((d_out, d_in), F32), full, full, full, full, full,
                pltpu.VMEM((reps, d_out // reps, d_in), BF),
                pltpu.VMEM((8, 128), F32), pltpu.VMEM((reps, 8, 128), F32), pltpu.VMEM(m.shape, F32),
                pltpu.SemaphoreType.DMA((n_copies,)), pltpu.SemaphoreType.DMA((n_copies,)),
                pltpu.SemaphoreType.DMA((6,)),
            ],
            compiler_params=pltpu.CompilerParams(collective_id=0, has_side_effects=True),
            name="kfac_step",
        )(g, inverse_out[0], inverse_in[0], cross_out[0], cross_in[0], m)
        return done[None]

    shared = P("layer", "rep", None)
    return jax.shard_map(
        body,
        mesh=mesh,
        in_specs=(P("rep", "layer", None, None), shared, shared, shared, shared, shared),
        out_specs=shared,
        check_vma=False,
    )
```

time: 202 us -> 82 us (0.41)
  the two profiles are of different devices: /device:TPU:2 before, /device:TPU:8 now
where the time goes in v1:
time: 82 us; the launch traced here: 81.9 us
  Pallas kernels  80.2 us (98%)
  local copies, waits for them, and re-layouts  1.67 us (2%)
    pallas_call x1, Pallas kernels, body(): pl.pallas_call(functools.partial(kernel, layers, reps), out_shape=jax.Sha...  80.2 us
    unnamed x1, local copies, waits for them, and re-layouts  1.67 us

profile of v1, /device:TPU:8, one launch (start us, length us, event | category | flops | bytes accessed | tf_op | source)
XLA Modules:
  0.0 81.9 jit_solution(16632647424067264403)
XLA Ops:
  0.0 80.2 %kfac_step.1 = f32[64,1024]{1,0:T(8,128)} custom-call(bf16[512,1024]{1,0:T(8,128)(2,1)} %bitcast.8, bf16[64,512]{1,0:T(8,128)(2,1)} %bitcast.12, bf16[128,1024]{1,0:T(8,128)(2,1)} %bitcast.9, bf16[64,512]{1,0:T(8,128)(2,1)} %bitcast.13, bf16[128,1024]{1,0:T(8,128)(2,1)} %bitcast.10, f32[64,1024]{1,0:T(8,128)} %bitcast.11), custom_call_target="tpu_custom_call" | custom-call | tf_op jit(solution)/shard_map/kfac_step/pallas_call | solution.py:300
  80.2 1.7 %copy.8 = f32[1,64,1024]{2,1,0:T(8,128)} copy(f32[1,64,1024]{2,1,0:T(8,128)} %bitcast.7) | data formatting | bytes 524288

commit v2 on v1

v2 whole, which is shorter than its diff:
```python
import contextlib
import functools

import jax
import jax.numpy as jnp
from jax import lax
from jax.experimental import pallas as pl
from jax.experimental.pallas import tpu as pltpu
from jax.sharding import PartitionSpec as P

MESH = pl.DeviceIdType.MESH
RING = 4
CHUNKS = 4
CUT = {"x": 4, "y": 4, "o": 4, "i": 5}
BF = jnp.bfloat16
F32 = jnp.float32


def phase(name):
    return contextlib.nullcontext()


def relay_layers(layers):
    quarter = layers // 2 // CHUNKS
    return {c: quarter * (c + 1) + 1 for c in range(CHUNKS - 1)}


def dot(a, b):
    return jnp.dot(a, b, preferred_element_type=F32)


def dot_t(a, b):
    return lax.dot_general(a, b, (((1,), (1,)), ((), ())), preferred_element_type=F32)


def kernel(
    layers, reps, own_g, sh_o, sh_i, sh_x, sh_y, out,
    f_x, f_y, f_o, f_i, xt, g_own, g_next, first, resid, left, acc, pre, back, corr, inc, ub, rb,
    sc_out, sc_in, hold, res, send, recv, loc,
):
    layer, rep = lax.axis_index("layer"), lax.axis_index("rep")
    y, xh = rep // 2, rep % 2
    d_out, d_in = g_own.shape
    slab = d_out // reps

    def slot_of(dy, other):
        return ((y + dy + RING) % RING) * 2 + ((1 - xh) if other else xh)

    up, down, across = (layer, slot_of(1, False)), (layer, slot_of(-1, False)), (layer, slot_of(0, True))

    local = []

    def bring(src, dst):
        c = pltpu.make_async_copy(src, dst, loc.at[len(local)])
        c.start()
        local.append(c)

    arrays = {"x": (sh_x, f_x), "y": (sh_y, f_y), "o": (sh_o, f_o), "i": (sh_i, f_i)}

    def rows_of(q, slot, part=None):
        shard, full = arrays[q]
        n = shard.shape[0]
        cols = full.shape[1]
        cut = cols * CUT[q] // 8
        lo, size = {"a": (0, cut), "b": (cut, cols - cut), None: (0, cols)}[part]
        return n, lo, size

    def full_at(q, slot, part, half=None):
        n, lo, size = rows_of(q, slot, part)
        start, count = (0, n) if half is None else (half * (n // 2), n // 2)
        at = pl.multiple_of(slot * n + start, count)
        return arrays[q][1].at[pl.ds(at, count), pl.ds(lo, size)]

    def own_at(q, part):
        n, lo, size = rows_of(q, None, part)
        return arrays[q][0].at[pl.ds(0, n), pl.ds(lo, size)]

    for q in arrays:
        bring(arrays[q][0], full_at(q, rep, None))
    bring(own_g, g_own)

    has_next = (layer + 1) // layers
    has_prev = (layer + layers - 1) // layers
    barrier = pltpu.get_barrier_semaphore()
    for k in range(1, reps):
        pl.semaphore_signal(barrier, inc=1, device_id=(layer, (rep + k) % reps), device_id_type=MESH)

    @pl.when(layer < layers - 1)
    def _():
        pl.semaphore_signal(barrier, inc=1, device_id=(layer + 1, rep), device_id_type=MESH)

    @pl.when(layer > 0)
    def _():
        pl.semaphore_signal(barrier, inc=1, device_id=(layer - 1, rep), device_id_type=MESH)

    half = layers // 2
    relays = relay_layers(layers)
    for at in relays.values():

        @pl.when(layer == at)
        def _():
            pl.semaphore_signal(barrier, inc=1, device_id=(half, rep), device_id_type=MESH)

    @pl.when(layer == half)
    def _():
        for k in range(1, reps):
            to = (half - 1, (rep + k) % reps)
            pl.semaphore_signal(barrier, inc=1, device_id=to, device_id_type=MESH)

    def is_layer(v):
        return (layer + layers - v) // layers - (layer + layers - v - 1) // layers

    extra = is_layer(half) * len(relays) + is_layer(half - 1) * (reps - 1)
    pl.semaphore_wait(barrier, reps - 1 + (1 - has_next) + has_prev + extra)

    tile = d_in // CHUNKS
    copies, out_at, in_at = {}, {}, {}
    last_in = ("bx0", "bx1", "bx2", "aur", "adr", "bx3", "bx4", "pur", "pdr")

    def index(table, key):
        return table.setdefault(key, len(table))

    def sender(key):
        return key[0] if key[0] in ("x", "y", "o", "i", "u", "s") else key

    def arrival(key):
        if key[0] in ("u", "s"):
            return key[0]
        if key[0] in ("x", "y", "o") and key[1] in last_in:
            return (key[0], "last")
        if key[0] == "i" and key[1] in ("bx1", "bx2"):
            return (key[0], "near")
        if key[0] == "i" and key[1] in last_in[3:]:
            return (key[0], "last")
        return key

    def remote(key, src, dst, device, arrives=None):
        c = pltpu.make_async_remote_copy(
            src_ref=src, dst_ref=dst, send_sem=send.at[index(out_at, sender(key))],
            recv_sem=recv.at[index(in_at, arrives or arrival(key))],
            device_id=device, device_id_type=MESH,
        )
        copies.setdefault(key, c)
        return c

    def await_bytes(sem, ref):
        pltpu.make_async_copy(ref, ref, sem).wait()

    def got_all(name, ref):
        await_bytes(recv.at[in_at[name]], ref)

    def sent_all(name, ref):
        await_bytes(send.at[out_at[name]], ref)

    for c in range(CHUNKS):
        index(in_at, ("c", c))

    def chunk(c):
        return pl.ds(c * tile, tile)

    def to_neighbour(name, c, src, dst, step, far, relays, near=True, beyond=True):
        end = layers - 1 if step > 0 else 0
        straight = remote((name, c), src, dst, (jnp.clip(layer + step, 0, layers - 1), rep))
        detour = remote((name, c), src, hold, (relays[c], rep), (name, "r")) if c in relays else straight
        if near:

            @pl.when((layer != end) & (layer != far))
            def _():
                straight.start()

        if beyond:

            @pl.when(layer == far)
            def _():
                detour.start()

    def relay(name, dst, step, far, relays, which):
        for c in which:
            onward = remote((name, "r"), hold, dst.at[:, chunk(c)], (far + step, rep), (name, c))

            @pl.when(layer == relays[c])
            def _(onward=onward):
                remote((name, "in"), hold, hold, (far + step, rep), (name, "r")).wait_recv()
                onward.start()
                onward.wait_send()

    def put(key, src, dst, device):
        remote(key, src, dst, device).start()

    def got(*keys):
        for key in keys:
            copies[key].wait_recv()

    def begin(q):
        put((q, "ax"), own_at(q, "a"), full_at(q, rep, "a"), across)
        put((q, "bx0"), own_at(q, "b"), full_at(q, rep, "b"), across)
        put((q, "bu"), own_at(q, "b"), full_at(q, rep, "b"), up)
        put((q, "bd"), own_at(q, "b"), full_at(q, rep, "b"), down)
        put((q, "au"), own_at(q, "a"), full_at(q, rep, "a"), up)
        put((q, "ad"), own_at(q, "a"), full_at(q, rep, "a"), down)

    def pass_on(q, name, slot, part, device, half=None):
        ref = full_at(q, slot, part, half)
        put((q, name), ref, ref, device)

    def stage1(q):
        got((q, "bu"))
        pass_on(q, "bur", slot_of(-1, False), "b", up, 0)
        pass_on(q, "bx1", slot_of(-1, False), "b", across)
        got((q, "bd"))
        pass_on(q, "bdr", slot_of(1, False), "b", down, 1)
        pass_on(q, "bx2", slot_of(1, False), "b", across)
        got((q, "ax"))
        pass_on(q, "pu", slot_of(0, True), "a", up)
        pass_on(q, "pd", slot_of(0, True), "a", down)

    def stage2(q):
        got((q, "au"))
        pass_on(q, "aur", slot_of(-1, False), "a", up, 0)
        got((q, "ad"))
        pass_on(q, "adr", slot_of(1, False), "a", down, 1)
        got((q, "bur"))
        pass_on(q, "bx3", slot_of(2, False), "b", across, 0)
        got((q, "bdr"))
        pass_on(q, "bx4", slot_of(2, False), "b", across, 1)

    def stage3(q):
        got((q, "pu"))
        pass_on(q, "pur", slot_of(-1, True), "a", up, 0)
        got((q, "pd"))
        pass_on(q, "pdr", slot_of(1, True), "a", down, 1)

    def finish(q):
        n = arrays[q][0].shape[0]
        got_all((q, "last"), arrays[q][1].at[pl.ds(0, 2 * n + n * (8 - CUT[q]) // 4), :])

    def each_tile(body):
        @pl.loop(0, CHUNKS)
        def _(n):
            body(pl.ds(pl.multiple_of(n * tile, tile), tile))

    with phase("begin"):
        for c in range(CHUNKS):
            to_neighbour("g", c, own_g.at[:, chunk(c)], g_next.at[:, chunk(c)], -1, half, relays, near=False)
        for q in "xyo":
            begin(q)
        for c in range(CHUNKS):
            to_neighbour("g", c, own_g.at[:, chunk(c)], g_next.at[:, chunk(c)], -1, half, relays, beyond=False)
    with phase("s1x"):
        stage1("x")
    with phase("s1y"):
        stage1("y")
    with phase("s1o"):
        stage1("o")
    with phase("s2x"):
        stage2("x")
    with phase("s3x"):
        stage3("x")
    with phase("s2y"):
        stage2("y")
    with phase("begin_i"):
        begin("i")
    with phase("s3y"):
        stage3("y")
    with phase("s2o"):
        stage2("o")
    with phase("s3o"):
        stage3("o")
    with phase("relay"):
        relay("g", g_next, -1, half, relays, relays)
    with phase("s1i"):
        stage1("i")
    for c in local:
        c.wait()
    with phase("fx"):
        finish("x")
    with phase("xt"):
        xt[...] = f_x[...].T

    with phase("gn"):

        @pl.when(layer < layers - 1)
        def _():
            for c in range(CHUNKS):
                copies[("g", c)].wait_recv()

        @pl.when(layer == layers - 1)
        def _():
            g_next[...] = jnp.zeros_like(g_next)

    def step1(cols):
        first[:, cols] = dot(f_x[...], g_next[:, cols]).astype(BF)

    with phase("st1"):
        each_tile(step1)
    with phase("fy"):
        finish("y")

    def step2(cols):
        resid[:, cols] = (g_own[:, cols].astype(F32) - dot(first[...], f_y[:, cols])).astype(BF)

    with phase("st2"):
        each_tile(step2)
    with phase("s2i"):
        stage2("i")
    with phase("fo"):
        finish("o")

    def step3(cols):
        left[:, cols] = dot(f_o[...], resid[:, cols]).astype(BF)

    with phase("st3"):
        each_tile(step3)
    with phase("s3i"):
        stage3("i")

    depth = 2 * sh_i.shape[0]

    def part(dy):
        return pl.ds(pl.multiple_of(((y + dy + RING) % RING) * depth, depth), depth)

    with phase("gi0"):
        got(("i", "bx0"))

    def step4_own(cols):
        acc[:, cols] = dot(left[:, part(0)], f_i[part(0), cols])

    with phase("st4a"):
        each_tile(step4_own)
    with phase("gi1"):
        n, _, rest = rows_of("i", None, "b")
        got_all(("i", "near"), f_i.at[pl.ds(0, 2 * n), pl.ds(0, rest)])

    def step4_near(cols):
        acc[:, cols] += dot(left[:, part(-1)], f_i[part(-1), cols]) + dot(left[:, part(1)], f_i[part(1), cols])

    with phase("st4b"):
        each_tile(step4_near)
    with phase("gi2"):
        got_all(("i", "last"), f_i.at[pl.ds(0, n + n * CUT["i"] // 8), :])

    def step4_far(cols):
        pre[:, cols] = (acc[:, cols] + dot(left[:, part(2)], f_i[part(2), cols])).astype(BF)

    with phase("st4c"):
        each_tile(step4_far)

    def step5(cols):
        back[:, cols] = dot(xt[...], pre[:, cols]).astype(BF)

    with phase("st5"):
        each_tile(step5)

    def rows_from(r):
        return pl.ds(pl.multiple_of(r * slab, slab), slab)

    def to_owners(name, src, dst):
        for k in range(1, reps):
            to = (rep + k) % reps
            put((name, k), src(to), dst, (layer, to))

    @pl.when(layer == half)
    def _():
        to_owners("u", lambda to: pre.at[rows_from(to), :], rb.at[rep])

    with phase("st6"):
        for c in range(CHUNKS):
            corr[:, chunk(c)] = dot_t(back[...], f_y[chunk(c), :]).astype(BF)
            src, dst = corr.at[:, chunk(c)], inc.at[:, chunk(c)]
            to_neighbour("c", c, src, dst, 1, half - 1, {}, beyond=False)

            @pl.when(layer == half - 1)
            def _(c=c):
                for k in range(reps):
                    to = (rep + k) % reps
                    there = inc.at[rows_from(rep), chunk(c)]
                    remote(("c", c), corr.at[rows_from(to), chunk(c)], there, (half, to)).start()

    @pl.when(layer == 0)
    def _():
        inc[...] = jnp.zeros_like(inc)

    for c in range(CHUNKS):
        with phase(f"inc{c}"):

            @pl.when(layer > 0)
            def _(c=c):
                copies[("c", c)].wait_recv()

        @pl.when(layer != half)
        def _(c=c):
            update = pre[:, chunk(c)].astype(F32) - inc[:, chunk(c)].astype(F32)
            ub[:, chunk(c)] = update.astype(BF)
            part = jnp.broadcast_to(jnp.sum(update * update, keepdims=True), sc_out.shape)
            total = part if c == 0 else sc_out[...] + part
            if c < CHUNKS - 1:
                sc_out[...] = total
            else:
                sc_out[...] = lax.rsqrt(total * (1.0 / (d_out * d_in)) + 1e-06)
                to_owners("s", lambda to: sc_out, sc_in.at[rep])
            to_owners("u", lambda to: ub.at[rows_from(to), chunk(c)], rb.at[rep, :, chunk(c)])

    others = reps - 1

    @pl.when(layer != half)
    def _():
        rb[rep] = ub[rows_from(rep), :]

    @pl.when(layer == half)
    def _():
        rb[rep] = pre[rows_from(rep), :]
        got_all("u", rb.at[pl.ds(0, others)])
        for r in range(reps):
            apart = rb[r].astype(F32) - inc[r * slab : (r + 1) * slab, :].astype(F32)
            acc[r * slab : (r + 1) * slab, :] = apart
            sc_out[r : r + 1, :] = jnp.broadcast_to(jnp.sum(apart * apart, keepdims=True), (1, 128))
        to_owners("s", lambda to: sc_out, sc_in.at[rep])

    with phase("sent"):
        sc_in[rep] = sc_out[...]
        for key, c in copies.items():
            if key[0] == "g" and key[1] not in ("r", "in"):
                pl.when(layer > 0)(c.wait_send)
            elif key[0] == "c":
                pl.when(layer < layers - 1)(c.wait_send)
        for q, (shard, full) in arrays.items():
            sent_all(q, full.at[pl.ds(0, others * shard.shape[0]), :])
        sent_all("s", sc_in.at[pl.ds(0, others)])
        sent_all("u", rb.at[pl.ds(0, others)])
    with phase("gots"):
        got_all("s", sc_in.at[pl.ds(0, others)])

    @pl.when(layer != half)
    def _():
        with phase("gotu"):
            got_all("u", rb.at[pl.ds(0, others)])
        with phase("sum"):
            share = rb[0].astype(F32) * sc_in[0, 0:1, 0:1]
            for r in range(1, reps):
                share = share + rb[r].astype(F32) * sc_in[r, 0:1, 0:1]
            res[...] = share * (1.0 / reps)

    @pl.when(layer == half)
    def _():
        squares = sc_in[0]
        for r in range(1, reps):
            squares = squares + sc_in[r]
        sc_out[...] = lax.rsqrt(squares * (1.0 / (d_out * d_in)) + 1e-06)
        share = acc[0:slab, :] * sc_out[0:1, 0:1]
        for r in range(1, reps):
            share = share + acc[r * slab : (r + 1) * slab, :] * sc_out[r : r + 1, 0:1]
        res[...] = share * (1.0 / reps)

    with phase("put_out"):
        c = pltpu.make_async_copy(res, out, loc.at[0])
        c.start()
        c.wait()


def solution(mesh):
    layers, reps = mesh.shape["layer"], mesh.shape["rep"]

    def body(gradients, inverse_out, inverse_in, cross_out, cross_in, momentum):
        g, m = gradients[0, 0], momentum[0]
        d_out, d_in = g.shape
        n_copies = 56
        full = pltpu.VMEM((d_out, d_in), BF)
        small, large = pltpu.VMEM((d_out, d_out), BF), pltpu.VMEM((d_in, d_in), BF)
        done = pl.pallas_call(
            functools.partial(kernel, layers, reps),
            out_shape=jax.ShapeDtypeStruct(m.shape, F32),
            in_specs=[pl.BlockSpec(memory_space=pl.ANY)] * 5,
            out_specs=pl.BlockSpec(memory_space=pl.ANY),
            scratch_shapes=[
                small, large, small, large, small,
                full, full, full, full, full, pltpu.VMEM((d_out, d_in), F32), full, full, full, full, full,
                pltpu.VMEM((reps, d_out // reps, d_in), BF),
                pltpu.VMEM((8, 128), F32), pltpu.VMEM((reps, 8, 128), F32), pltpu.VMEM((d_out, d_in // CHUNKS), BF),
                pltpu.VMEM(m.shape, F32),
                pltpu.SemaphoreType.DMA((18,)), pltpu.SemaphoreType.DMA((n_copies,)),
                pltpu.SemaphoreType.DMA((5,)),
            ],
            compiler_params=pltpu.CompilerParams(collective_id=0, has_side_effects=True),
            name="kfac_step",
        )(g, inverse_out[0], inverse_in[0], cross_out[0], cross_in[0])
        return (0.9 * m + done)[None]

    shared = P("layer", "rep", None)
    return jax.shard_map(
        body,
        mesh=mesh,
        in_specs=(P("rep", "layer", None, None), shared, shared, shared, shared, shared),
        out_specs=shared,
        check_vma=False,
    )
```

time: 82 us -> 75.8 us (0.924)
  the two profiles are of different devices: /device:TPU:8 before, /device:TPU:2 now
where the time goes in v2:
time: 75.8 us; the launch traced here: 75.7 us
  Pallas kernels  74 us (98%)
  other arithmetic  1.69 us (2%)
    pallas_call x1, Pallas kernels, body(): pl.pallas_call(functools.partial(kernel, layers, reps), out_shape=jax.Sha...  74 us
    broadcast_in_dim x1, other arithmetic, body(): return (0.9 * m + done)[None]  1.69 us

profile of v2, /device:TPU:2, one launch (start us, length us, event | category | flops | bytes accessed | tf_op | source)
XLA Modules:
  0.0 75.7 jit_solution(8199206252967259828)
XLA Ops:
  0.0 0.0 copy-start
  0.0 74.0 %kfac_step.1 = f32[64,1024]{1,0:T(8,128)} custom-call(bf16[512,1024]{1,0:T(8,128)(2,1)} %bitcast.11, bf16[64,512]{1,0:T(8,128)(2,1)} %bitcast.14, bf16[128,1024]{1,0:T(8,128)(2,1)} %bitcast.12, bf16[64,512]{1,0:T(8,128)(2,1)} %bitcast.15, bf16[128,1024]{1,0:T(8,128)(2,1)} %bitcast.13), custom_call_target="tpu_custom_call" | custom-call | tf_op jit(solution)/shard_map/kfac_step/pallas_call | solution.py:469
  74.0 0.0 copy-done
  74.0 1.7 %fusion = f32[1,64,1024]{2,1,0:T(8,128)} fusion(f32[64,1024]{1,0:T(8,128)} %kfac_step.1, f32[1,64,1024]{2,1,0:T(8,128)S(1)} %copy-done), kind=kLoop, calls=%fused_computation.1 | loop fusion | flops 131072 | bytes 786432 | tf_op jit(solution)/shard_map/broadcast_in_dim | solution.py:486
Async XLA Ops:
  0.0 74.0 %copy-start = (f32[1,64,1024]{2,1,0:T(8,128)S(1)}, f32[1,64,1024]{2,1,0:T(8,128)}, u32[]{:S(2)}) copy-start(f32[1,64,1024]{2,1,0:T(8,128)} %param.11) | copy-start | bytes 786436

commit v3 on v2

--- a/solution.py
+++ b/solution.py
@@ -36,7 +36,7 @@
 def kernel(
     layers, reps, own_g, sh_o, sh_i, sh_x, sh_y, out,
     f_x, f_y, f_o, f_i, xt, g_own, g_next, first, resid, left, acc, pre, back, corr, inc, ub, rb,
-    sc_out, sc_in, hold, res, send, recv, loc,
+    sc_out, sc_in, hold, send, recv, loc,
 ):
     layer, rep = lax.axis_index("layer"), lax.axis_index("rep")
     y, xh = rep // 2, rep % 2
@@ -73,7 +73,7 @@
 
     def own_at(q, part):
         n, lo, size = rows_of(q, None, part)
-        return arrays[q][0].at[pl.ds(0, n), pl.ds(lo, size)]
+        return full_at(q, rep, part)
 
     for q in arrays:
         bring(arrays[q][0], full_at(q, rep, None))
@@ -107,11 +107,18 @@
             to = (half - 1, (rep + k) % reps)
             pl.semaphore_signal(barrier, inc=1, device_id=to, device_id_type=MESH)
 
+    @pl.when(layer == layers - 1)
+    def _():
+        pl.semaphore_signal(barrier, inc=1, device_id=(half - 1, rep), device_id_type=MESH)
+
     def is_layer(v):
         return (layer + layers - v) // layers - (layer + layers - v - 1) // layers
 
-    extra = is_layer(half) * len(relays) + is_layer(half - 1) * (reps - 1)
+    extra = is_layer(half) * len(relays) + is_layer(half - 1) * reps
     pl.semaphore_wait(barrier, reps - 1 + (1 - has_next) + has_prev + extra)
+
+    for c in local[:4]:
+        c.wait()
 
     tile = d_in // CHUNKS
     copies, out_at, in_at = {}, {}, {}
@@ -270,7 +277,7 @@
         relay("g", g_next, -1, half, relays, relays)
     with phase("s1i"):
         stage1("i")
-    for c in local:
+    for c in local[4:]:
         c.wait()
     with phase("fx"):
         finish("x")
@@ -363,6 +370,11 @@
     def _():
         to_owners("u", lambda to: pre.at[rows_from(to), :], rb.at[rep])
 
+    def to_far_owners(key, src, c):
+        for k in range(reps):
+            to = (rep + k) % reps
+            remote(key, src(to), inc.at[rows_from(rep), chunk(c)], (half, to), ("c", c)).start()
+
     with phase("st6"):
         for c in range(CHUNKS):
             corr[:, chunk(c)] = dot_t(back[...], f_y[chunk(c), :]).astype(BF)
@@ -371,19 +383,26 @@
 
             @pl.when(layer == half - 1)
             def _(c=c):
-                for k in range(reps):
-                    to = (rep + k) % reps
-                    there = inc.at[rows_from(rep), chunk(c)]
-                    remote(("c", c), corr.at[rows_from(to), chunk(c)], there, (half, to)).start()
+                if c == 0:
+                    remote(("c", 0), corr.at[:, chunk(0)], hold, (layers - 1, rep), ("c", "r")).start()
+                else:
+                    to_far_owners(("c", c), lambda to: corr.at[rows_from(to), chunk(c)], c)
 
     @pl.when(layer == 0)
     def _():
         inc[...] = jnp.zeros_like(inc)
+
+    with phase("relay_c"):
+
+        @pl.when(layer == layers - 1)
+        def _():
+            got_all(("c", "r"), hold)
+            to_far_owners(("c", "r"), lambda to: hold.at[rows_from(to), :], 0)
 
     for c in range(CHUNKS):
         with phase(f"inc{c}"):
 
-            @pl.when(layer > 0)
+            @pl.when((layer > 0) & (layer != half))
             def _(c=c):
                 copies[("c", c)].wait_recv()
 
@@ -410,10 +429,15 @@
     def _():
         rb[rep] = pre[rows_from(rep), :]
         got_all("u", rb.at[pl.ds(0, others)])
-        for r in range(reps):
-            apart = rb[r].astype(F32) - inc[r * slab : (r + 1) * slab, :].astype(F32)
-            acc[r * slab : (r + 1) * slab, :] = apart
-            sc_out[r : r + 1, :] = jnp.broadcast_to(jnp.sum(apart * apart, keepdims=True), (1, 128))
+        order = [*range(1, CHUNKS), 0]
+        for c in order:
+            with phase(f"far{c}"):
+                copies[("c", c)].wait_recv()
+            for r in range(reps):
+                apart = rb[r, :, chunk(c)].astype(F32) - inc[r * slab : (r + 1) * slab, chunk(c)].astype(F32)
+                acc[r * slab : (r + 1) * slab, chunk(c)] = apart
+                squares = jnp.broadcast_to(jnp.sum(apart * apart, keepdims=True), (1, 128))
+                sc_out[r : r + 1, :] = squares if c == order[0] else sc_out[r : r + 1, :] + squares
         to_owners("s", lambda to: sc_out, sc_in.at[rep])
 
     with phase("sent"):
@@ -421,11 +445,16 @@
         for key, c in copies.items():
             if key[0] == "g" and key[1] not in ("r", "in"):
                 pl.when(layer > 0)(c.wait_send)
-            elif key[0] == "c":
+            elif key[0] == "c" and key[1] != "r":
                 pl.when(layer < layers - 1)(c.wait_send)
         for q, (shard, full) in arrays.items():
             sent_all(q, full.at[pl.ds(0, others * shard.shape[0]), :])
         sent_all("s", sc_in.at[pl.ds(0, others)])
+
+        @pl.when(layer == layers - 1)
+        def _():
+            sent_all(("c", "r"), hold)
+
         sent_all("u", rb.at[pl.ds(0, others)])
     with phase("gots"):
         got_all("s", sc_in.at[pl.ds(0, others)])
@@ -438,7 +467,7 @@
             share = rb[0].astype(F32) * sc_in[0, 0:1, 0:1]
             for r in range(1, reps):
                 share = share + rb[r].astype(F32) * sc_in[r, 0:1, 0:1]
-            res[...] = share * (1.0 / reps)
+            out[...] = share * (1.0 / reps)
 
     @pl.when(layer == half)
     def _():
@@ -449,12 +478,7 @@
         share = acc[0:slab, :] * sc_out[0:1, 0:1]
         for r in range(1, reps):
             share = share + acc[r * slab : (r + 1) * slab, :] * sc_out[r : r + 1, 0:1]
-        res[...] = share * (1.0 / reps)
-
-    with phase("put_out"):
-        c = pltpu.make_async_copy(res, out, loc.at[0])
-        c.start()
-        c.wait()
+        out[...] = share * (1.0 / reps)
 
 
 def solution(mesh):
@@ -468,15 +492,14 @@
         small, large = pltpu.VMEM((d_out, d_out), BF), pltpu.VMEM((d_in, d_in), BF)
         done = pl.pallas_call(
             functools.partial(kernel, layers, reps),
-            out_shape=jax.ShapeDtypeStruct(m.shape, F32),
+            out_shape=pltpu.VMEM(m.shape, F32),
             in_specs=[pl.BlockSpec(memory_space=pl.ANY)] * 5,
-            out_specs=pl.BlockSpec(memory_space=pl.ANY),
+            out_specs=pl.BlockSpec(memory_space=pltpu.VMEM),
             scratch_shapes=[
                 small, large, small, large, small,
                 full, full, full, full, full, pltpu.VMEM((d_out, d_in), F32), full, full, full, full, full,
                 pltpu.VMEM((reps, d_out // reps, d_in), BF),
                 pltpu.VMEM((8, 128), F32), pltpu.VMEM((reps, 8, 128), F32), pltpu.VMEM((d_out, d_in // CHUNKS), BF),
-                pltpu.VMEM(m.shape, F32),
                 pltpu.SemaphoreType.DMA((18,)), pltpu.SemaphoreType.DMA((n_copies,)),
                 pltpu.SemaphoreType.DMA((5,)),
             ],

time: 75.8 us -> 73.2 us (0.966)
  Pallas kernels: 74 us -> 72.3 us
  other arithmetic: 1.69 us -> 0.74 us
    pallas_call x1, Pallas kernels: 74 us -> 72.3 us  [body(): pl.pallas_call(functools.partial(kernel, layers, reps), out_shape=pltpu.V...]
    broadcast_in_dim x1, other arithmetic: 1.69 us -> 0.74 us  [body(): return (0.9 * m + done)[None]]
where the time goes in v3:
time: 73.2 us; the launch traced here: 73.1 us
  Pallas kernels  72.3 us (99%)
  other arithmetic  0.74 us (1%)
    pallas_call x1, Pallas kernels, body(): pl.pallas_call(functools.partial(kernel, layers, reps), out_shape=pltpu.V...  72.3 us

profile of v3, /device:TPU:2, one launch (start us, length us, event | category | flops | bytes accessed | tf_op | source)
XLA Modules:
  0.0 73.1 jit_solution(9801953539253265260)
XLA Ops:
  0.0 0.0 copy-start
  0.0 72.3 %kfac_step.1 = f32[64,1024]{1,0:T(8,128)S(1)} custom-call(bf16[512,1024]{1,0:T(8,128)(2,1)} %bitcast.11, bf16[64,512]{1,0:T(8,128)(2,1)} %bitcast.14, bf16[128,1024]{1,0:T(8,128)(2,1)} %bitcast.12, bf16[64,512]{1,0:T(8,128)(2,1)} %bitcast.15, bf16[128,1024]{1,0:T(8,128)(2,1)} %bitcast.13), custom_call_target="tpu_custom_call" | custom-call | tf_op jit(solution)/shard_map/kfac_step/pallas_call | solution.py:493
  72.3 0.0 copy-done
  72.3 0.7 %fusion = f32[1,64,1024]{2,1,0:T(8,128)} fusion(f32[64,1024]{1,0:T(8,128)S(1)} %kfac_step.1, f32[1,64,1024]{2,1,0:T(8,128)S(1)} %copy-done), kind=kLoop, calls=%fused_computation.1 | loop fusion | flops 131072 | bytes 786432 | tf_op jit(solution)/shard_map/broadcast_in_dim | solution.py:509
Async XLA Ops:
  0.0 72.3 %copy-start = (f32[1,64,1024]{2,1,0:T(8,128)S(1)}, f32[1,64,1024]{2,1,0:T(8,128)}, u32[]{:S(2)}) copy-start(f32[1,64,1024]{2,1,0:T(8,128)} %param.11) | copy-start | bytes 786436

commit v4 on v3

--- a/solution.py
+++ b/solution.py
@@ -36,7 +36,7 @@
 def kernel(
     layers, reps, own_g, sh_o, sh_i, sh_x, sh_y, out,
     f_x, f_y, f_o, f_i, xt, g_own, g_next, first, resid, left, acc, pre, back, corr, inc, ub, rb,
-    sc_out, sc_in, hold, send, recv, loc,
+    sc_out, sc_in, hold, send, recv, loc, turn,
 ):
     layer, rep = lax.axis_index("layer"), lax.axis_index("rep")
     y, xh = rep // 2, rep % 2
@@ -399,6 +399,12 @@
             got_all(("c", "r"), hold)
             to_far_owners(("c", "r"), lambda to: hold.at[rows_from(to), :], 0)
 
+    with phase("turn"):
+
+        @pl.when(layer == half + 1)
+        def _():
+            pl.semaphore_wait(turn, 1)
+
     for c in range(CHUNKS):
         with phase(f"inc{c}"):
 
@@ -429,6 +435,7 @@
     def _():
         rb[rep] = pre[rows_from(rep), :]
         got_all("u", rb.at[pl.ds(0, others)])
+        pl.semaphore_signal(turn, inc=1, device_id=(half + 1, rep), device_id_type=MESH)
         order = [*range(1, CHUNKS), 0]
         for c in order:
             with phase(f"far{c}"):
@@ -501,7 +508,7 @@
                 pltpu.VMEM((reps, d_out // reps, d_in), BF),
                 pltpu.VMEM((8, 128), F32), pltpu.VMEM((reps, 8, 128), F32), pltpu.VMEM((d_out, d_in // CHUNKS), BF),
                 pltpu.SemaphoreType.DMA((18,)), pltpu.SemaphoreType.DMA((n_copies,)),
-                pltpu.SemaphoreType.DMA((5,)),
+                pltpu.SemaphoreType.DMA((5,)), pltpu.SemaphoreType.REGULAR,
             ],
             compiler_params=pltpu.CompilerParams(collective_id=0, has_side_effects=True),
             name="kfac_step",

time: 73.2 us -> 71.3 us (0.974)
  Pallas kernels: 72.3 us -> 70.4 us
    pallas_call x1, Pallas kernels: 72.3 us -> 70.4 us  [body(): pl.pallas_call(functools.partial(kernel, layers, reps), out_shape=pltpu.V...]
where the time goes in v4:
time: 71.3 us; the launch traced here: 71.2 us
  Pallas kernels  70.4 us (99%)
  other arithmetic  0.74 us (1%)
    pallas_call x1, Pallas kernels, body(): pl.pallas_call(functools.partial(kernel, layers, reps), out_shape=pltpu.V...  70.4 us

profile of v4, /device:TPU:2, one launch (start us, length us, event | category | flops | bytes accessed | tf_op | source)
XLA Modules:
  0.0 71.2 jit_solution(1675373828413783501)
XLA Ops:
  0.0 0.0 copy-start
  0.0 70.4 %kfac_step.1 = f32[64,1024]{1,0:T(8,128)S(1)} custom-call(bf16[512,1024]{1,0:T(8,128)(2,1)} %bitcast.11, bf16[64,512]{1,0:T(8,128)(2,1)} %bitcast.14, bf16[128,1024]{1,0:T(8,128)(2,1)} %bitcast.12, bf16[64,512]{1,0:T(8,128)(2,1)} %bitcast.15, bf16[128,1024]{1,0:T(8,128)(2,1)} %bitcast.13), custom_call_target="tpu_custom_call" | custom-call | tf_op jit(solution)/shard_map/kfac_step/pallas_call | solution.py:500
  70.4 0.0 copy-done
  70.5 0.7 %fusion = f32[1,64,1024]{2,1,0:T(8,128)} fusion(f32[64,1024]{1,0:T(8,128)S(1)} %kfac_step.1, f32[1,64,1024]{2,1,0:T(8,128)S(1)} %copy-done), kind=kLoop, calls=%fused_computation.1 | loop fusion | flops 131072 | bytes 786432 | tf_op jit(solution)/shard_map/broadcast_in_dim | solution.py:516
Async XLA Ops:
  0.0 70.5 %copy-start = (f32[1,64,1024]{2,1,0:T(8,128)S(1)}, f32[1,64,1024]{2,1,0:T(8,128)}, u32[]{:S(2)}) copy-start(f32[1,64,1024]{2,1,0:T(8,128)} %param.11) | copy-start | bytes 786436
